TPU v7x, 32 devices: a whole 2x2x4 slice. The times are simulated.
32 devices in a mesh: seq: 8 (over y, x, core), req: 4 (over z).
Axes of the slice: x: 2, y: 2, z: 4, core: 2. Of those that a mesh axis runs over, the one named last changes fastest.
Arguments:
- queries: bfloat16 [8, 256, 1536], P('req', 'seq'), as said below
- new_kv: bfloat16 [2, 8, 256, 512], P(None, 'req', 'seq'), may hold values from -6 to 6
- cache_kv: bfloat16 [2, 8, 2048, 512], P(None, 'req', 'seq'), as said below
- cache_spans: int32 [8, 2], P('req'), may hold values from 0 to 2048, as said below
- recompute_rows: int32 [8, 256], P('req'), may hold values from 0 to 2047, as said below
- held_states: bfloat16 [8, 256, 1536], P('req', 'seq'), may hold values from -6 to 6
- key_weight: bfloat16 [1536, 512], replicated, may hold values from -0.15625 to 0.15625
- norm_gain: float32 [1536], replicated, may hold values from 0.1 to 1.9
- routes: int32 [8, 256, 8], P('req', 'seq'), may hold values from 0 to 19, all different within a row; in each aligned block of 32 rows (0 to 31, 32 to 63, ..., all dimensions but the last counted through in order) at most 16 rows name the same one
- route_weights: float32 [8, 256, 8], P('req', 'seq'), may hold values from 0.05 to 1
- expert_gate_up: bfloat16 [20, 1536, 1024], P('req'), may hold values from -0.15625 to 0.15625
- expert_down: bfloat16 [20, 512, 1536], P('req'), may hold values from -0.25 to 0.25
Outputs:
- layer_out: bfloat16 [8, 256, 1536], P('req', 'seq')
Inputs may be any that keep to these rules, and one draw needn't show every extreme that they name: `routes`: in each aligned block of 32 rows of one request (one device's rows of that request) no expert is named more than 16 times. cache_spans[r] = (start, length): 1024 <= length <= 2048 with some request of length 2048; 0 <= start <= 512 with some request starting at 0. `recompute_rows`: within a request the rows are distinct and lie between the request's start and length. `queries`: entries lie within -6 to 6. `cache_kv`: entries lie within -6 to 6.
All inputs are finite; a program needn't handle non-finite values.
Results may differ from a plain program's by a relative error of at most 0.034.
Values may be sent and summed in bfloat16 or wider, within the bound.
A program may use at most 192 MiB of HBM per device.

v0:
```python
import jax
import jax.numpy as jnp
from jax import lax
from jax.sharding import PartitionSpec as P

H = 24
KVH = 8
HD = 64
FF = 512
TOP = 8
CAP = 16
NEG = -1e30
THETA = 10000.0


def rotate(key_heads, positions):
    half_dim = key_heads.shape[-1] // 2
    exponent = jnp.arange(half_dim).astype(jnp.float32) * (2.0 / key_heads.shape[-1])
    inverse = THETA ** (-exponent)
    angles = positions.astype(jnp.float32)[..., None] * inverse
    cosine = jnp.cos(angles)[..., None, :]
    sine_part = jnp.sin(angles)[..., None, :]
    lower_half = key_heads[..., :half_dim]
    upper_half = key_heads[..., half_dim:]
    return jnp.concatenate(
        [
            lower_half * cosine - upper_half * sine_part,
            upper_half * cosine + lower_half * sine_part,
        ],
        axis=-1,
    )


def partial_attend(packed):
    query_rows, key_rows, value_rows, allowed = packed
    query_count, model_width = query_rows.shape
    key_count = key_rows.shape[0]
    groups = H // KVH
    query_heads = query_rows.reshape(query_count, KVH, groups, HD)
    key_heads = key_rows.reshape(key_count, KVH, HD)
    value_heads = value_rows.reshape(key_count, KVH, HD)
    scores = jnp.einsum(
        "qkgd,nkd->kgqn", query_heads, key_heads, preferred_element_type=jnp.float32
    ) * HD ** (-0.5)
    scores = jnp.where(allowed[None, None, :, :], scores, NEG)
    highest = jnp.max(scores, axis=-1, keepdims=True)
    exps = jnp.exp(scores - highest)
    totals = jnp.sum(exps, axis=-1)
    weights = exps.astype(jnp.bfloat16)
    mixed_rows = jnp.einsum(
        "kgqn,nkd->qkgd", weights, value_heads, preferred_element_type=jnp.float32
    )
    mixed_rows = mixed_rows / jnp.transpose(totals, (2, 0, 1))[..., None]
    log_total = highest[..., 0] + jnp.log(totals)
    log_rows = jnp.transpose(log_total, (2, 0, 1)).reshape(query_count, H)
    return (mixed_rows.reshape(query_count, model_width), log_rows)


def body_wide(
    queries,
    new_kv,
    cache_kv,
    cache_spans,
    recompute_rows,
    held_states,
    key_weight,
    norm_gain,
    routes,
    route_weights,
    expert_gate_up,
    expert_down,
):
    seq_index = lax.axis_index("seq")
    seq_count = lax.axis_size("seq")
    owner_count = lax.axis_size("req")
    req_rows, tok_rows, model_width = queries.shape
    cache_rows = cache_kv.shape[2]
    held_rows = held_states.shape[1]
    local_experts = expert_gate_up.shape[0]
    expert_total = owner_count * local_experts
    my_positions = lax.dynamic_slice_in_dim(recompute_rows, seq_index * held_rows, held_rows, 1)
    projected = jnp.dot(
        held_states.reshape(req_rows * held_rows, model_width),
        key_weight,
        preferred_element_type=jnp.float32,
    )
    rotated = rotate(projected.reshape(req_rows, held_rows, KVH, HD), my_positions)
    rotated = rotated.reshape(req_rows, held_rows, KVH * HD).astype(jnp.bfloat16)
    fresh_rows = lax.all_gather(rotated, "seq", axis=1, tiled=True)
    cache_positions = seq_index * cache_rows + jnp.arange(cache_rows)
    hit_table = recompute_rows[:, None, :] == cache_positions[None, :, None]
    placed = jnp.einsum(
        "rcm,rmk->rck",
        hit_table.astype(jnp.bfloat16),
        fresh_rows,
        preferred_element_type=jnp.float32,
    ).astype(jnp.bfloat16)
    cache_keys = jnp.where(jnp.any(hit_table, axis=2)[:, :, None], placed, cache_kv[0])
    span_start = cache_spans[:, 0:1]
    span_end = cache_spans[:, 1:2]
    all_queries = lax.all_gather(queries, "seq", axis=1, tiled=True)
    step_total = all_queries.shape[1]
    cache_allowed = (cache_positions[None, :] >= span_start) & (cache_positions[None, :] < span_end)
    key_positions = seq_index * tok_rows + jnp.arange(tok_rows)
    step_allowed = key_positions[None, :] <= jnp.arange(step_total)[:, None]
    allowed = jnp.concatenate(
        [
            jnp.broadcast_to(cache_allowed[:, None, :], (req_rows, step_total, cache_rows)),
            jnp.broadcast_to(step_allowed[None], (req_rows, step_total, tok_rows)),
        ],
        axis=2,
    )
    key_rows = jnp.concatenate([cache_keys, new_kv[0]], axis=1)
    value_rows = jnp.concatenate([cache_kv[1], new_kv[1]], axis=1)
    part_out, part_log = lax.map(partial_attend, (all_queries, key_rows, value_rows, allowed))
    piece_out, piece_log = (
        lax.all_to_all(part_out[None], "seq", split_axis=2, concat_axis=0, tiled=True),
        lax.all_to_all(part_log[None], "seq", split_axis=2, concat_axis=0, tiled=True),
    )
    best_log = jnp.max(piece_log, axis=0)
    factors = jnp.exp(piece_log - best_log[None])
    factor_sum = jnp.sum(factors, axis=0)
    spread_out = piece_out.reshape(seq_count, req_rows, tok_rows, H, HD)
    combined = jnp.sum(spread_out * factors[..., None], axis=0) / factor_sum[..., None]
    attended_f = combined.reshape(req_rows, tok_rows, model_width)
    attended = attended_f.astype(jnp.bfloat16)
    attended_f = attended.astype(jnp.float32)
    mean_square = jnp.mean(attended_f * attended_f, axis=-1, keepdims=True)
    normed = (attended_f * lax.rsqrt(mean_square + 1e-06) * norm_gain).astype(jnp.bfloat16)
    route_flat = routes.reshape(req_rows, tok_rows * TOP)
    expert_match = (route_flat[:, :, None] == jnp.arange(expert_total)[None, None, :]).astype(
        jnp.int32
    )
    earlier = jnp.cumsum(expert_match, axis=1) - expert_match
    slot_index = jnp.sum(earlier * expert_match, axis=2)
    target = route_flat * CAP + slot_index
    slot_match = target[:, :, None] == jnp.arange(expert_total * CAP)[None, None, :]
    dispatch = jnp.any(
        slot_match.reshape(req_rows, tok_rows, TOP, expert_total * CAP), axis=2
    ).astype(jnp.bfloat16)
    dispatch = dispatch.reshape(req_rows, tok_rows, owner_count, local_experts, CAP)
    outgoing = jnp.einsum(
        "rtnec,rtd->nrecd", dispatch, normed, preferred_element_type=jnp.float32
    ).astype(jnp.bfloat16)
    hidden = jnp.einsum(
        "srecd,edf->srecf",
        lax.all_to_all(outgoing, "req", split_axis=0, concat_axis=0, tiled=True),
        expert_gate_up,
        preferred_element_type=jnp.float32,
    )
    active = (jax.nn.silu(hidden[..., :FF]) * hidden[..., FF:]).astype(jnp.bfloat16)
    result = jnp.einsum(
        "srecf,efd->srecd", active, expert_down, preferred_element_type=jnp.float32
    ).astype(jnp.bfloat16)
    returned = lax.all_to_all(result, "req", split_axis=0, concat_axis=0, tiled=True)
    owner_of = route_flat // local_experts
    local_of = route_flat % local_experts
    flat_index = (
        (owner_of * req_rows + jnp.arange(req_rows)[:, None]) * local_experts + local_of
    ) * CAP + slot_index
    returned_rows = jnp.take(returned.reshape(-1, model_width), flat_index.reshape(-1), axis=0)
    returned_rows = returned_rows.reshape(req_rows, tok_rows, TOP, model_width)
    mixture = jnp.einsum(
        "rtk,rtkd->rtd",
        route_weights,
        returned_rows.astype(jnp.float32),
        precision=lax.Precision.HIGHEST,
    )
    return (attended_f + mixture).astype(jnp.bfloat16)


def head_parallel_body(
    queries,
    new_kv,
    cache_kv,
    cache_spans,
    recompute_rows,
    held_states,
    key_weight,
    norm_gain,
    routes,
    route_weights,
    expert_gate_up,
    expert_down,
):
    seq_index = lax.axis_index("seq")
    seq_count = lax.axis_size("seq")
    req_index = lax.axis_index("req")
    owner_count = lax.axis_size("req")
    req_rows, tok_rows, model_width = queries.shape
    cache_rows = cache_kv.shape[2]
    held_rows = held_states.shape[1]
    local_experts = expert_gate_up.shape[0]
    groups = H // KVH
    bf16 = jnp.bfloat16
    f32 = jnp.float32
    my_positions = lax.dynamic_slice_in_dim(recompute_rows, seq_index * held_rows, held_rows, 1)
    projected = jnp.dot(
        held_states.reshape(req_rows * held_rows, model_width),
        key_weight,
        preferred_element_type=f32,
    )
    rotated = rotate(projected.reshape(req_rows, held_rows, KVH, HD), my_positions).astype(bf16)
    kv = jnp.concatenate([cache_kv, new_kv], axis=2)
    kv = kv.reshape(2, req_rows, cache_rows + tok_rows, KVH, HD).transpose(3, 1, 2, 0, 4)
    kv = kv.reshape(KVH, req_rows, cache_rows + tok_rows, 2 * HD)
    kv = lax.all_to_all(kv, "seq", split_axis=0, concat_axis=0, tiled=True)
    query_pack = queries.reshape(req_rows, tok_rows, KVH, groups * HD).transpose(2, 0, 1, 3)
    query_pack = lax.all_to_all(query_pack, "seq", split_axis=0, concat_axis=0, tiled=True)
    fresh = lax.all_to_all(
        rotated.transpose(2, 0, 1, 3), "seq", split_axis=0, concat_axis=0, tiled=True
    )
    fresh = fresh.transpose(1, 0, 2, 3).reshape(req_rows, seq_count * held_rows, HD)
    cache_total = seq_count * cache_rows
    step_total = seq_count * tok_rows
    cache_part = kv[:, :, :cache_rows].transpose(1, 0, 2, 3).reshape(req_rows, cache_total, 2 * HD)
    step_part = kv[:, :, cache_rows:].transpose(1, 0, 2, 3).reshape(req_rows, step_total, 2 * HD)
    positions = jnp.arange(cache_total)
    hit_table = recompute_rows[:, None, :] == positions[None, :, None]
    placed = jnp.einsum(
        "rcm,rmk->rck", hit_table.astype(bf16), fresh, preferred_element_type=f32
    ).astype(bf16)
    cache_keys = jnp.where(jnp.any(hit_table, axis=2)[:, :, None], placed, cache_part[..., :HD])
    keys = jnp.concatenate([cache_keys, step_part[..., :HD]], axis=1)
    values = jnp.concatenate([cache_part[..., HD:], step_part[..., HD:]], axis=1)
    heads = query_pack.reshape(seq_count, req_rows, tok_rows, groups, HD).transpose(1, 3, 0, 2, 4)
    heads = heads.reshape(req_rows, groups, step_total, HD)
    scores = jnp.einsum("rgqd,rnd->rgqn", heads, keys, preferred_element_type=f32) * HD ** (-0.5)
    cache_allowed = (positions[None] >= cache_spans[:, 0:1]) & (
        positions[None] < cache_spans[:, 1:2]
    )
    step_allowed = jnp.arange(step_total)[None, :] <= jnp.arange(step_total)[:, None]
    allowed = jnp.concatenate(
        [
            jnp.broadcast_to(cache_allowed[:, None, :], (req_rows, step_total, cache_total)),
            jnp.broadcast_to(step_allowed[None], (req_rows, step_total, step_total)),
        ],
        axis=2,
    )
    scores = jnp.where(allowed[:, None], scores, NEG)
    exps = jnp.exp(scores - jnp.max(scores, axis=-1, keepdims=True))
    totals = jnp.sum(exps, axis=-1, keepdims=True)
    mixed = jnp.einsum("rgqn,rnd->rgqd", exps.astype(bf16), values, preferred_element_type=f32)
    mixed = (mixed / totals).astype(bf16)
    mixed = mixed.reshape(req_rows, groups, seq_count, tok_rows, HD).transpose(2, 0, 3, 1, 4)
    mixed = mixed.reshape(seq_count, req_rows, tok_rows, groups * HD)
    mixed = lax.all_to_all(mixed, "seq", split_axis=0, concat_axis=0, tiled=True)
    attended = mixed.transpose(1, 2, 0, 3).reshape(req_rows * tok_rows, model_width)
    attended_f = attended.astype(f32)
    mean_square = jnp.mean(attended_f * attended_f, axis=-1, keepdims=True)
    normed = (attended_f * lax.rsqrt(mean_square + 1e-06) * norm_gain).astype(bf16)
    tokens = lax.all_gather(normed, "req", axis=0, tiled=True)
    all_routes = lax.all_gather(routes.reshape(req_rows * tok_rows, TOP), "req", axis=0, tiled=True)
    all_weights = lax.all_gather(
        route_weights.reshape(req_rows * tok_rows, TOP), "req", axis=0, tiled=True
    )
    mine = req_index * local_experts + jnp.arange(local_experts)
    share = jnp.sum(
        jnp.where(all_routes[:, :, None] == mine[None, None], all_weights[:, :, None], 0.0), axis=1
    )
    total = jnp.zeros(tokens.shape, f32)
    for e in range(local_experts):
        hidden = jnp.dot(tokens, expert_gate_up[e], preferred_element_type=f32)
        active = (jax.nn.silu(hidden[:, :FF]) * hidden[:, FF:]).astype(bf16)
        result = jnp.dot(active, expert_down[e], preferred_element_type=f32).astype(bf16)
        total = total + result.astype(f32) * share[:, e : e + 1]
    pieces = total.astype(bf16).reshape(owner_count, req_rows * tok_rows, model_width)
    pieces = lax.all_to_all(pieces, "req", split_axis=0, concat_axis=0, tiled=True)
    mixture = jnp.sum(pieces.astype(f32), axis=0)
    return (attended_f + mixture).astype(bf16).reshape(req_rows, tok_rows, model_width)


def solution(mesh):
    body = head_parallel_body if mesh.shape["seq"] == KVH else body_wide
    in_specs = (
        P("req", "seq", None),
        P(None, "req", "seq", None),
        P(None, "req", "seq", None),
        P("req", None),
        P("req", None),
        P("req", "seq", None),
        P(),
        P(),
        P("req", "seq", None),
        P("req", "seq", None),
        P("req", None, None),
        P("req", None, None),
    )
    out_specs = P("req", "seq", None)
    return jax.shard_map(body, mesh=mesh, in_specs=in_specs, out_specs=out_specs, check_vma=False)
```

profile of v0, /device:TPU:0, one launch (start us, length us, event | category | flops | bytes accessed | tf_op | source)
XLA Modules:
  0.0 173.9 jit_solution(13547308417040345744)
XLA Ops:
  0.0 1.8 %copy.124 = bf16[1536,512]{0,1:T(8,128)(2,1)S(1)} copy(bf16[1536,512]{1,0:T(8,128)(2,1)} %param.18) | data formatting | bytes 3145728 | tf_op args[6]
  2.1 0.9 fusion.78
  3.3 0.8 reshape.168
  4.1 5.2 %all-to-all-start = ((bf16[8,2,2048]{2,1,0:T(2,128)(2,1)}), bf16[8,2,2048]{2,1,0:T(2,128)(2,1)S(1)}, u32[]{:S(2)}, u32[]{:S(2)}) async-start(bf16[8,2,2048]{2,1,0:T(2,128)(2,1)} %reshape.168), calls=%async_computation | async-start | bytes 131072 | tf_op jit(solution)/shard_map/all_to_all | solution.py:210
  9.4 13.3 %all-gather.1 = f32[4,64,8]{1,2,0:T(8,128)S(1)} all-gather(f32[1,64,8]{1,2,0:T(8,128)S(1)} %reshape.158), channel_id=1, replica_groups=mesh['seq'=8,'req'=4] {'req'}, dimensions={0}, use_global_device_ids=true | all-gather | bytes 10240 | tf_op jit(solution)/shard_map/all_gather | solution.py:254
  22.9 13.1 %all-gather = s32[4,64,8]{1,2,0:T(8,128)S(1)} all-gather(s32[1,64,8]{1,2,0:T(8,128)S(1)} %reshape.156), channel_id=1, replica_groups=mesh['seq'=8,'req'=4] {'req'}, dimensions={0}, use_global_device_ids=true | all-gather | bytes 10240 | tf_op jit(solution)/shard_map/all_gather | solution.py:253
  36.1 0.2 reshape.146
  36.3 0.8 copy.158
  37.1 0.3 copy.129
  37.4 0.5 copy.128
  38.3 1.6 copy.131
  39.9 4.2 %all-to-all-start.2 = ((bf16[8,2,32,192]{3,2,1,0:T(8,128)(2,1)}), bf16[8,2,32,192]{3,2,1,0:T(8,128)(2,1)S(1)}, u32[]{:S(2)}, u32[]{:S(2)}) async-start(bf16[8,2,32,192]{3,2,1,0:T(8,128)(2,1)} %bitcast.120), calls=%async_computation.2 | async-start | bytes 524288 | tf_op jit(solution)/shard_map/all_to_all | solution.py:209
  44.2 6.8 %all-to-all-done.2 = bf16[8,2,32,192]{3,2,1,0:T(8,128)(2,1)S(1)} async-done(((bf16[8,2,32,192]{3,2,1,0:T(8,128)(2,1)}), bf16[8,2,32,192]{3,2,1,0:T(8,128)(2,1)S(1)}, u32[]{:S(2)}, u32[]{:S(2)}) %all-to-all-start.2) | async-done | bytes 196640 | tf_op jit(solution)/shard_map/all_to_all | solution.py:209
  51.0 3.7 %all-to-all-start.1 = ((bf16[8,2,288,128]{3,2,1,0:T(8,128)(2,1)}), bf16[8,2,288,128]{3,2,1,0:T(8,128)(2,1)S(1)}, u32[]{:S(2)}, u32[]{:S(2)}) async-start(bf16[8,2,288,128]{3,2,1,0:T(8,128)(2,1)} %copy.131), calls=%async_computation.1 | async-start | bytes 2359296 | tf_op jit(solution)/shard_map/all_to_all | solution.py:207
  54.9 0.6 fusion.7
  55.7 0.8 broadcast_in_dim.28
  56.6 0.4 pad_add_fusion
  57.1 0.7 copy.126
  58.0 13.3 %all-to-all-done.1 = bf16[8,2,288,128]{3,2,1,0:T(8,128)(2,1)S(1)} async-done(((bf16[8,2,288,128]{3,2,1,0:T(8,128)(2,1)}), bf16[8,2,288,128]{3,2,1,0:T(8,128)(2,1)S(1)}, u32[]{:S(2)}, u32[]{:S(2)}) %all-to-all-start.1) | async-done | bytes 1179680 | tf_op jit(solution)/shard_map/all_to_all | solution.py:207
  71.3 1.1 slice_bitcast_fusion
  72.4 2.6 %copy.132 = bf16[2,8,256,128]{2,1,3,0:T(8,128)(2,1)} copy(bf16[2,8,256,128]{3,2,0,1:T(8,128)(2,1)} %slice_bitcast_fusion) | data formatting | bytes 2097152 | tf_op jit(solution)/shard_map/transpose | solution.py:216
  75.1 2.3 %reshape.144 = bf16[2,2048,128]{1,2,0:T(8,128)(2,1)} reshape(bf16[2,8,256,128]{2,1,3,0:T(8,128)(2,1)} %copy.132) | data formatting | bytes 2097152 | tf_op jit(solution)/shard_map/reshape | solution.py:216
  77.8 0.5 copy-done.6
  78.3 0.4 copy-done.2
  78.7 1.0 fusion.39
  79.7 6.4 %fusion.2 = (f32[2,3,256]{2,1,0:T(4,128)S(1)}, f32[2,2304,3,256]{3,1,2,0:T(8,128)}) fusion(pred[2,256,2304]{1,2,0:T(8,128)(4,1)S(1)} %pad_add_fusion, bf16[2,3,256,64]{3,2,1,0:T(8,128)(2,1)S(1)} %bitcast.129, bf16[2,256,64]{1,2,0:T(8,128)(2,1)S(1)} %copy.156, bf16[2,2048,64]{1,2,0:T(8,128)(2,1)S(1)} %fusion.39), kind=kOutput, calls=%fused_computation.4 | convolution fusion | flops 464779776 | bytes 16128000 | tf_op jit(solution)/shard_map/rgqd,rnd->rgqn/dot_general | solution.py:228
  86.1 8.1 %fusion = f32[2,3,256]{2,1,0:T(4,128)S(1)} fusion(f32[2,2304,3,256]{3,1,2,0:T(8,128)} %get-tuple-element.19, f32[2,3,256]{2,1,0:T(4,128)S(1)} %get-tuple-element.18, pred[2,256,2304]{1,2,0:T(8,128)(4,1)S(1)} %pad_add_fusion), kind=kLoop, calls=%fused_computation.2 | loop fusion | flops 14154240 | bytes 15347712 | tf_op jit(solution)/shard_map/reduce_sum | solution.py:242
  94.2 7.0 %fusion.54 = bf16[2,3,256,64]{2,3,1,0:T(8,128)(2,1)S(1)} fusion(f32[2,2304,3,256]{3,1,2,0:T(8,128)} %get-tuple-element.19, f32[2,3,256]{2,1,0:T(4,128)S(1)} %get-tuple-element.18, pred[2,256,2304]{1,2,0:T(8,128)(4,1)S(1)} %pad_add_fusion, bf16[2,256,64]{1,2,0:T(8,128)(2,1)S(1)} %copy.155, bf16[2,2048,64]{1,2,0:T(8,128)(2,1)S(1)} %slice-done, ...), kind=kOutput, calls=%fused_computation.63 | convolution fusion | flops 468516864 | bytes 16134144 | tf_op jit(solution)/shard_map/rgqn,rnd->rgqd/dot_general | solution.py:243
  101.3 0.2 copy.140
  101.5 0.3 copy.141
  101.9 1.0 reshape.150
  102.9 3.4 %all-to-all-start.3 = ((bf16[8,2,32,192]{3,2,1,0:T(8,128)(2,1)}), bf16[8,2,32,192]{3,2,1,0:T(8,128)(2,1)S(1)}, u32[]{:S(2)}, u32[]{:S(2)}) async-start(bf16[8,2,32,192]{3,2,1,0:T(8,128)(2,1)} %reshape.150), calls=%async_computation.3 | async-start | bytes 524288 | tf_op jit(solution)/shard_map/all_to_all | solution.py:247
  106.3 6.8 %all-to-all-done.3 = bf16[8,2,32,192]{3,2,1,0:T(8,128)(2,1)S(1)} async-done(((bf16[8,2,32,192]{3,2,1,0:T(8,128)(2,1)}), bf16[8,2,32,192]{3,2,1,0:T(8,128)(2,1)S(1)}, u32[]{:S(2)}, u32[]{:S(2)}) %all-to-all-start.3) | async-done | bytes 196640 | tf_op jit(solution)/shard_map/all_to_all | solution.py:247
  113.5 0.3 copy.142
  114.1 19.9 %all_gather.9 = bf16[256,1536]{1,0:T(8,128)(2,1)S(1)} all-gather(bf16[64,1536]{1,0:T(8,128)(2,1)S(1)} %multiply_convert_fusion), channel_id=1, replica_groups=mesh['seq'=8,'req'=4] {'req'}, dimensions={0}, use_global_device_ids=true | all-gather | bytes 983040 | tf_op jit(solution)/shard_map/all_gather | solution.py:252
  134.0 2.9 %fusion.8 = f32[256,1024]{1,0:T(8,128)S(1)} fusion(bf16[256,1536]{1,0:T(8,128)(2,1)S(1)} %all_gather.9, bf16[5,1536,1024]{2,1,0:T(8,128)(2,1)} %param.22), kind=kOutput, calls=%fused_computation.11 | convolution fusion | flops 805306368 | bytes 4980736 | tf_op jit(solution)/shard_map/dot_general | solution.py:263
  136.9 2.9 %fusion.10 = f32[256,1024]{1,0:T(8,128)S(1)} fusion(bf16[256,1536]{1,0:T(8,128)(2,1)S(1)} %all_gather.9, bf16[5,1536,1024]{2,1,0:T(8,128)(2,1)} %param.22), kind=kOutput, calls=%fused_computation.13 | convolution fusion | flops 805306368 | bytes 4980736 | tf_op jit(solution)/shard_map/dot_general | solution.py:263
  139.9 3.1 %fusion.12 = f32[256,1024]{1,0:T(8,128)S(1)} fusion(bf16[256,1536]{1,0:T(8,128)(2,1)S(1)} %all_gather.9, bf16[5,1536,1024]{2,1,0:T(8,128)(2,1)} %param.22), kind=kOutput, calls=%fused_computation.15 | convolution fusion | flops 805306368 | bytes 4980736 | tf_op jit(solution)/shard_map/dot_general | solution.py:263
  143.0 3.1 %fusion.14 = f32[256,1024]{1,0:T(8,128)S(1)} fusion(bf16[256,1536]{1,0:T(8,128)(2,1)S(1)} %all_gather.9, bf16[5,1536,1024]{2,1,0:T(8,128)(2,1)} %param.22), kind=kOutput, calls=%fused_computation.17 | convolution fusion | flops 805306368 | bytes 4980736 | tf_op jit(solution)/shard_map/dot_general | solution.py:263
  146.0 2.9 %fusion.16 = f32[256,1024]{1,0:T(8,128)S(1)} fusion(bf16[256,1536]{1,0:T(8,128)(2,1)S(1)} %all_gather.9, bf16[5,1536,1024]{2,1,0:T(8,128)(2,1)} %param.22), kind=kOutput, calls=%fused_computation.19 | convolution fusion | flops 805306368 | bytes 4980736 | tf_op jit(solution)/shard_map/dot_general | solution.py:263
  149.0 0.6 fusion.37
  149.6 0.6 fusion.35
  150.3 0.6 fusion.32
  150.9 0.6 fusion.29
  151.5 1.5 fusion.26
  153.0 3.5 %all-to-all-start.4 = ((bf16[4,64,1536]{2,1,0:T(8,128)(2,1)}), bf16[4,64,1536]{2,1,0:T(8,128)(2,1)S(1)}, u32[]{:S(2)}, u32[]{:S(2)}) async-start(bf16[4,64,1536]{2,1,0:T(8,128)(2,1)} %bitcast.41), calls=%async_computation.4 | async-start | bytes 1572864 | tf_op jit(solution)/shard_map/all_to_all | solution.py:268
  156.7 16.4 %all-to-all-done.4 = bf16[4,64,1536]{2,1,0:T(8,128)(2,1)S(1)} async-done(((bf16[4,64,1536]{2,1,0:T(8,128)(2,1)}), bf16[4,64,1536]{2,1,0:T(8,128)(2,1)S(1)}, u32[]{:S(2)}, u32[]{:S(2)}) %all-to-all-start.4) | async-done | bytes 786464 | tf_op jit(solution)/shard_map/all_to_all | solution.py:268
  173.2 0.7 add_convert_fusion
  (69 shorter events, 3.3 us)
Async XLA Ops:
  0.0 2.1 %copy-start = (bf16[2,32,1536]{2,1,0:T(8,128)(2,1)S(1)}, bf16[2,32,1536]{2,1,0:T(8,128)(2,1)}, u32[]{:S(2)}) copy-start(bf16[2,32,1536]{2,1,0:T(8,128)(2,1)} %param.17) | copy-start | bytes 589828
  0.0 1.8 %copy-start.10 = (s32[2,256]{1,0:T(2,128)S(1)}, s32[2,256]{1,0:T(2,128)}, u32[]{:S(2)}) copy-start(s32[2,256]{1,0:T(2,128)} %param.16) | copy-start | bytes 6148
  2.1 7.2 %copy-start.8 = (s32[2,32,8]{1,2,0:T(8,128)S(1)}, s32[2,32,8]{1,2,0:T(8,128)}, u32[]{:S(2)}) copy-start(s32[2,32,8]{1,2,0:T(8,128)} %param.20) | copy-start | bytes 6148
  2.1 7.3 %copy-start.9 = (f32[2,32,8]{1,2,0:T(8,128)S(1)}, f32[2,32,8]{1,2,0:T(8,128)}, u32[]{:S(2)}) copy-start(f32[2,32,8]{1,2,0:T(8,128)} %param.21) | copy-start | bytes 6148
  2.1 34.0 %copy-start.4 = (bf16[2,32,1536]{2,1,0:T(8,128)(2,1)S(1)}, bf16[2,32,1536]{2,1,0:T(8,128)(2,1)}, u32[]{:S(2)}) copy-start(bf16[2,32,1536]{2,1,0:T(8,128)(2,1)} %param.12) | copy-start | bytes 589828
  3.0 34.1 %copy-start.5 = (bf16[2,2,32,512]{3,2,1,0:T(8,128)(2,1)S(1)}, bf16[2,2,32,512]{3,2,1,0:T(8,128)(2,1)}, u32[]{:S(2)}) copy-start(bf16[2,2,32,512]{3,2,1,0:T(8,128)(2,1)} %param.13) | copy-start | bytes 393220
  3.1 34.2 %copy-start.3 = (bf16[2,2,256,512]{3,2,1,0:T(8,128)(2,1)S(1)}, bf16[2,2,256,512]{3,2,1,0:T(8,128)(2,1)}, u32[]{:S(2)}) copy-start(bf16[2,2,256,512]{3,2,1,0:T(8,128)(2,1)} %param.14) | copy-start | bytes 3145732
  4.1 35.8 %all-to-all-start = ((bf16[8,2,2048]{2,1,0:T(2,128)(2,1)}), bf16[8,2,2048]{2,1,0:T(2,128)(2,1)S(1)}, u32[]{:S(2)}, u32[]{:S(2)}) async-start(bf16[8,2,2048]{2,1,0:T(2,128)(2,1)} %reshape.168), calls=%async_computation | async-start | bytes 131072 | tf_op jit(solution)/shard_map/all_to_all | solution.py:210
  39.8 14.9 %copy-start.11 = (s32[2,2]{1,0:T(2,128)S(1)}, s32[2,2]{1,0:T(2,128)}, u32[]{:S(2)}) copy-start(s32[2,2]{1,0:T(2,128)} %param.15) | copy-start | bytes 52
  39.9 11.1 %all-to-all-start.2 = ((bf16[8,2,32,192]{3,2,1,0:T(8,128)(2,1)}), bf16[8,2,32,192]{3,2,1,0:T(8,128)(2,1)S(1)}, u32[]{:S(2)}, u32[]{:S(2)}) async-start(bf16[8,2,32,192]{3,2,1,0:T(8,128)(2,1)} %bitcast.120), calls=%async_computation.2 | async-start | bytes 524288 | tf_op jit(solution)/shard_map/all_to_all | solution.py:209
  51.0 20.3 %all-to-all-start.1 = ((bf16[8,2,288,128]{3,2,1,0:T(8,128)(2,1)}), bf16[8,2,288,128]{3,2,1,0:T(8,128)(2,1)S(1)}, u32[]{:S(2)}, u32[]{:S(2)}) async-start(bf16[8,2,288,128]{3,2,1,0:T(8,128)(2,1)} %copy.131), calls=%async_computation.1 | async-start | bytes 2359296 | tf_op jit(solution)/shard_map/all_to_all | solution.py:207
  77.4 0.9 copy-start.6
  77.4 1.3 copy-start.2
  86.1 8.1 %slice-start = ((bf16[2,2048,128]{1,2,0:T(8,128)(2,1)}), bf16[2,2048,64]{1,2,0:T(8,128)(2,1)S(1)}, s32[]{:S(2)}) async-start(bf16[2,2048,128]{1,2,0:T(8,128)(2,1)} %reshape.144), calls=%async_computation.5 | async-start | bytes 1048576 | tf_op jit(solution)/shard_map/slice | solution.py:225
  102.9 10.3 %all-to-all-start.3 = ((bf16[8,2,32,192]{3,2,1,0:T(8,128)(2,1)}), bf16[8,2,32,192]{3,2,1,0:T(8,128)(2,1)S(1)}, u32[]{:S(2)}, u32[]{:S(2)}) async-start(bf16[8,2,32,192]{3,2,1,0:T(8,128)(2,1)} %reshape.150), calls=%async_computation.3 | async-start | bytes 524288 | tf_op jit(solution)/shard_map/all_to_all | solution.py:247
  106.3 7.7 %copy-start.7 = (f32[1536]{0:T(1024)S(1)}, f32[1536]{0:T(1024)}, u32[]{:S(2)}) copy-start(f32[1536]{0:T(1024)} %param.19) | copy-start | bytes 18436
  139.9 9.1 %slice-start.1 = ((s8[7864320]{0:T(1024)(128)(4,1)}), s8[4194304]{0:T(1024)(128)(4,1)S(1)}, s32[]{:S(2)}) async-start(s8[7864320]{0:T(1024)(128)(4,1)} %bitcast.136), calls=%async_computation.6 | async-start | bytes 8388608
  142.9 6.1 %slice-start.2 = ((s8[7864320]{0:T(1024)(128)(4,1)}), s8[3670016]{0:T(1024)(128)(4,1)S(1)}, s32[]{:S(2)}) async-start(s8[7864320]{0:T(1024)(128)(4,1)} %bitcast.136), calls=%async_computation.7 | async-start | bytes 7340032
  153.0 20.1 %all-to-all-start.4 = ((bf16[4,64,1536]{2,1,0:T(8,128)(2,1)}), bf16[4,64,1536]{2,1,0:T(8,128)(2,1)S(1)}, u32[]{:S(2)}, u32[]{:S(2)}) async-start(bf16[4,64,1536]{2,1,0:T(8,128)(2,1)} %bitcast.41), calls=%async_computation.4 | async-start | bytes 1572864 | tf_op jit(solution)/shard_map/all_to_all | solution.py:268
  156.5 17.4 %copy-start.1 = (bf16[2,32,1536]{2,1,0:T(8,128)(2,1)S(1)}, bf16[2,32,1536]{2,1,0:T(8,128)(2,1)}, u32[]{:S(2)}) copy-start(bf16[2,32,1536]{2,1,0:T(8,128)(2,1)} %param.17) | copy-start | bytes 589828
where the time goes:
time: 175 us; the launch traced here: 174 us
  blocking collectives  46.4 us (27%)
  waiting for transfers between devices  43.3 us (25%)
  matrix products  34.2 us (20%)
  starting transfers between devices  20 us (11%)
  local copies, waits for them, and re-layouts  18.3 us (10%)
  other arithmetic  11.2 us (6%)
    all_gather x1, blocking collectives, head_parallel_body(): tokens = lax.all_gather(normed, 'req', axis=0, tiled=True)  19.9 us
    all_to_all x1, waiting for transfers between devices, head_parallel_body(): lax.all_to_all(pieces, 'req', split_axis=0, concat_axis=0, tiled=True)  16.4 us
    dot_general x5, matrix products, head_parallel_body(): hidden = jnp.dot(tokens, expert_gate_up[e], preferred_element_type=f32)  14.9 us
    all_gather x1, blocking collectives, head_parallel_body(): lax.all_gather(route_weights.reshape(req_rows * tok_rows, TOP), 'req', ax...  13.3 us
    all_to_all x1, waiting for transfers between devices, head_parallel_body(): kv = lax.all_to_all(kv, 'seq', split_axis=0, concat_axis=0, tiled=True)  13.3 us
    all_gather x1, blocking collectives, head_parallel_body(): lax.all_gather(routes.reshape(req_rows * tok_rows, TOP), 'req', axis=0, t...  13.1 us
    reduce_sum x1, other arithmetic, head_parallel_body(): totals = jnp.sum(exps, axis=-1, keepdims=True)  8.13 us
    dot_general x1, matrix products, head_parallel_body(): jnp.einsum('rgqn,rnd->rgqd', exps.astype(bf16), values, preferred_element...  7.03 us
  transfers between devices with their start and end apart: 5, of which 4 were waited for; matrix products, arithmetic and copies ran while one was open for 4% of the time, Pallas kernels for 0%

commit v1 on v0

--- a/solution.py
+++ b/solution.py
@@ -249,7 +249,12 @@
     attended_f = attended.astype(f32)
     mean_square = jnp.mean(attended_f * attended_f, axis=-1, keepdims=True)
     normed = (attended_f * lax.rsqrt(mean_square + 1e-06) * norm_gain).astype(bf16)
-    tokens = lax.all_gather(normed, "req", axis=0, tiled=True)
+    ring = [normed]
+    for hop in range(3):
+        ring.append(lax.ppermute(ring[-1], "req", [(dev, (dev + 1) % 4) for dev in range(4)]))
+    tokens = jnp.roll(
+        jnp.concatenate(ring[::-1], axis=0), (lax.axis_index("req") + 1) * ring[0].shape[0], axis=0
+    )
     all_routes = lax.all_gather(routes.reshape(req_rows * tok_rows, TOP), "req", axis=0, tiled=True)
     all_weights = lax.all_gather(
         route_weights.reshape(req_rows * tok_rows, TOP), "req", axis=0, tiled=True

time: 175 us -> 168 us (0.960)
  blocking collectives: 46.4 us -> 35.9 us
  waiting for transfers between devices: 43.3 us -> 50 us
  starting transfers between devices: 20 us -> 17.8 us
    all_gather x1 -> x0, blocking collectives: 19.9 us -> none  [head_parallel_body(): tokens = lax.all_gather(normed, 'req', axis=0, tiled=True)]
    ppermute x0 -> x3, waiting for transfers between devices: none -> 15.8 us  [head_parallel_body(): lax.ppermute(ring[-1], 'req', [(dev, (dev + 1) % 4) for dev in range(4)])]
    all_to_all x0 -> x1, blocking collectives: none -> 9.34 us  [head_parallel_body(): lax.all_to_all(mixed, 'seq', split_axis=0, concat_axis=0, tiled=True)]
    all_to_all x1 -> x0, waiting for transfers between devices: 6.84 us -> none  [head_parallel_body(): lax.all_to_all(mixed, 'seq', split_axis=0, concat_axis=0, tiled=True)]
    all_to_all x1, waiting for transfers between devices: 16.4 us -> 12.9 us  [head_parallel_body(): lax.all_to_all(pieces, 'req', split_axis=0, concat_axis=0, tiled=True)]
    all_to_all x1 -> x0, starting transfers between devices: 3.41 us -> none  [head_parallel_body(): lax.all_to_all(mixed, 'seq', split_axis=0, concat_axis=0, tiled=True)]
    all_to_all x1, waiting for transfers between devices: 0.01 us -> 3.18 us  [head_parallel_body(): lax.all_to_all(rotated.transpose(2, 0, 1, 3), 'seq', split_axis=0, concat...]
    ppermute x0 -> x3, starting transfers between devices: none -> 1.98 us  [head_parallel_body(): lax.ppermute(ring[-1], 'req', [(dev, (dev + 1) % 4) for dev in range(4)])]
  transfers between devices with their start and end apart: 5 -> 7, of which waited for: 4 -> 6; matrix products, arithmetic and copies ran while one was open for 4% -> 4% of each run, Pallas kernels for 0% -> 0%
where the time goes in v1:
time: 168 us
  waiting for transfers between devices  50 us (30%)
  blocking collectives  35.9 us (21%)
  matrix products  34.2 us (20%)
  starting transfers between devices  17.8 us (11%)
  local copies, waits for them, and re-layouts  17.6 us (10%)
  other arithmetic  11.4 us (7%)
    ppermute x3, waiting for transfers between devices, head_parallel_body(): lax.ppermute(ring[-1], 'req', [(dev, (dev + 1) % 4) for dev in range(4)])  15.8 us
    dot_general x5, matrix products, head_parallel_body(): hidden = jnp.dot(tokens, expert_gate_up[e], preferred_element_type=f32)  15 us
    all_gather x1, blocking collectives, head_parallel_body(): lax.all_gather(route_weights.reshape(req_rows * tok_rows, TOP), 'req', ax...  13.4 us
    all_to_all x1, waiting for transfers between devices, head_parallel_body(): kv = lax.all_to_all(kv, 'seq', split_axis=0, concat_axis=0, tiled=True)  13.3 us
    all_gather x1, blocking collectives, head_parallel_body(): lax.all_gather(routes.reshape(req_rows * tok_rows, TOP), 'req', axis=0, t...  13.2 us
    all_to_all x1, waiting for transfers between devices, head_parallel_body(): lax.all_to_all(pieces, 'req', split_axis=0, concat_axis=0, tiled=True)  12.9 us
    all_to_all x1, blocking collectives, head_parallel_body(): lax.all_to_all(mixed, 'seq', split_axis=0, concat_axis=0, tiled=True)  9.34 us
    reduce_sum x1, other arithmetic, head_parallel_body(): totals = jnp.sum(exps, axis=-1, keepdims=True)  8.13 us
  transfers between devices with their start and end apart: 7, of which 6 were waited for; matrix products, arithmetic and copies ran while one was open for 4% of the time, Pallas kernels for 0%

profile of v1, /device:TPU:0, one launch (start us, length us, event | category | flops | bytes accessed | tf_op | source)
XLA Modules:
  0.0 167.6 jit_solution(3517085314132425523)
XLA Ops:
  0.0 1.8 %copy.124 = bf16[1536,512]{0,1:T(8,128)(2,1)S(1)} copy(bf16[1536,512]{1,0:T(8,128)(2,1)} %param.18) | data formatting | bytes 3145728 | tf_op args[6]
  2.1 0.9 fusion.83
  3.3 0.8 reshape.168
  4.1 5.2 %all-to-all-start = ((bf16[8,2,2048]{2,1,0:T(2,128)(2,1)}), bf16[8,2,2048]{2,1,0:T(2,128)(2,1)S(1)}, u32[]{:S(2)}, u32[]{:S(2)}) async-start(bf16[8,2,2048]{2,1,0:T(2,128)(2,1)} %reshape.168), calls=%async_computation | async-start | bytes 131072 | tf_op jit(solution)/shard_map/all_to_all | solution.py:210
  9.5 0.8 copy.158
  10.3 0.3 copy.129
  10.5 0.5 copy.128
  11.1 3.2 %all-to-all-done = bf16[8,2,2048]{2,1,0:T(2,128)(2,1)S(1)} async-done(((bf16[8,2,2048]{2,1,0:T(2,128)(2,1)}), bf16[8,2,2048]{2,1,0:T(2,128)(2,1)S(1)}, u32[]{:S(2)}, u32[]{:S(2)}) %all-to-all-start) | async-done | bytes 65568 | tf_op jit(solution)/shard_map/all_to_all | solution.py:210
  14.3 3.4 %all-to-all-start.2 = ((bf16[8,2,32,192]{3,2,1,0:T(8,128)(2,1)}), bf16[8,2,32,192]{3,2,1,0:T(8,128)(2,1)S(1)}, u32[]{:S(2)}, u32[]{:S(2)}) async-start(bf16[8,2,32,192]{3,2,1,0:T(8,128)(2,1)} %bitcast.115), calls=%async_computation.2 | async-start | bytes 524288 | tf_op jit(solution)/shard_map/all_to_all | solution.py:209
  18.0 1.6 copy.131
  19.6 4.9 %all-to-all-done.2 = bf16[8,2,32,192]{3,2,1,0:T(8,128)(2,1)S(1)} async-done(((bf16[8,2,32,192]{3,2,1,0:T(8,128)(2,1)}), bf16[8,2,32,192]{3,2,1,0:T(8,128)(2,1)S(1)}, u32[]{:S(2)}, u32[]{:S(2)}) %all-to-all-start.2) | async-done | bytes 196640 | tf_op jit(solution)/shard_map/all_to_all | solution.py:209
  24.5 3.7 %all-to-all-start.1 = ((bf16[8,2,288,128]{3,2,1,0:T(8,128)(2,1)}), bf16[8,2,288,128]{3,2,1,0:T(8,128)(2,1)S(1)}, u32[]{:S(2)}, u32[]{:S(2)}) async-start(bf16[8,2,288,128]{3,2,1,0:T(8,128)(2,1)} %copy.131), calls=%async_computation.1 | async-start | bytes 2359296 | tf_op jit(solution)/shard_map/all_to_all | solution.py:207
  28.5 0.6 fusion.7
  29.3 0.8 broadcast_in_dim.28
  30.1 0.4 pad_add_fusion
  30.7 0.7 copy.126
  31.5 13.3 %all-to-all-done.1 = bf16[8,2,288,128]{3,2,1,0:T(8,128)(2,1)S(1)} async-done(((bf16[8,2,288,128]{3,2,1,0:T(8,128)(2,1)}), bf16[8,2,288,128]{3,2,1,0:T(8,128)(2,1)S(1)}, u32[]{:S(2)}, u32[]{:S(2)}) %all-to-all-start.1) | async-done | bytes 1179680 | tf_op jit(solution)/shard_map/all_to_all | solution.py:207
  44.9 1.1 slice_bitcast_fusion
  46.0 2.6 %copy.132 = bf16[2,8,256,128]{2,1,3,0:T(8,128)(2,1)} copy(bf16[2,8,256,128]{3,2,0,1:T(8,128)(2,1)} %slice_bitcast_fusion) | data formatting | bytes 2097152 | tf_op jit(solution)/shard_map/transpose | solution.py:216
  48.6 2.3 %reshape.144 = bf16[2,2048,128]{1,2,0:T(8,128)(2,1)} reshape(bf16[2,8,256,128]{2,1,3,0:T(8,128)(2,1)} %copy.132) | data formatting | bytes 2097152 | tf_op jit(solution)/shard_map/reshape | solution.py:216
  51.3 0.5 copy-done.6
  51.8 0.4 copy-done.2
  52.2 1.0 fusion.39
  53.2 6.4 %fusion.2 = (f32[2,3,256]{2,1,0:T(4,128)S(1)}, f32[2,2304,3,256]{3,1,2,0:T(8,128)}) fusion(pred[2,256,2304]{1,2,0:T(8,128)(4,1)S(1)} %pad_add_fusion, bf16[2,3,256,64]{3,2,1,0:T(8,128)(2,1)S(1)} %bitcast.124, bf16[2,256,64]{1,2,0:T(8,128)(2,1)S(1)} %copy.156, bf16[2,2048,64]{1,2,0:T(8,128)(2,1)S(1)} %fusion.39), kind=kOutput, calls=%fused_computation.4 | convolution fusion | flops 464779776 | bytes 16128000 | tf_op jit(solution)/shard_map/rgqd,rnd->rgqn/dot_general | solution.py:228
  59.6 8.1 %fusion = f32[2,3,256]{2,1,0:T(4,128)S(1)} fusion(f32[2,2304,3,256]{3,1,2,0:T(8,128)} %get-tuple-element.19, f32[2,3,256]{2,1,0:T(4,128)S(1)} %get-tuple-element.18, pred[2,256,2304]{1,2,0:T(8,128)(4,1)S(1)} %pad_add_fusion), kind=kLoop, calls=%fused_computation.2 | loop fusion | flops 14154240 | bytes 15347712 | tf_op jit(solution)/shard_map/reduce_sum | solution.py:242
  67.8 7.0 %fusion.54 = bf16[2,3,256,64]{2,3,1,0:T(8,128)(2,1)S(1)} fusion(f32[2,2304,3,256]{3,1,2,0:T(8,128)} %get-tuple-element.19, f32[2,3,256]{2,1,0:T(4,128)S(1)} %get-tuple-element.18, pred[2,256,2304]{1,2,0:T(8,128)(4,1)S(1)} %pad_add_fusion, bf16[2,256,64]{1,2,0:T(8,128)(2,1)S(1)} %copy.155, bf16[2,2048,64]{1,2,0:T(8,128)(2,1)S(1)} %slice-done, ...), kind=kOutput, calls=%fused_computation.63 | convolution fusion | flops 468516864 | bytes 16134144 | tf_op jit(solution)/shard_map/rgqn,rnd->rgqd/dot_general | solution.py:243
  75.0 0.3 copy.141
  75.4 0.3 reshape.150
  75.7 9.3 %all_to_all.25 = bf16[8,2,32,192]{3,2,1,0:T(8,128)(2,1)S(1)} all-to-all(bf16[8,2,32,192]{3,2,1,0:T(8,128)(2,1)S(1)} %reshape.150), channel_id=1, replica_groups=mesh['seq'=8,'req'=4] {'seq'}, dimensions={0} | all-to-all | bytes 393216 | tf_op jit(solution)/shard_map/all_to_all | solution.py:247
  85.3 0.3 copy.142
  85.9 1.9 %collective-permute-start = (bf16[64,1536]{1,0:T(8,128)(2,1)S(1)}, bf16[64,1536]{1,0:T(8,128)(2,1)S(1)}, u32[]{:S(2)}, u32[]{:S(2)}) collective-permute-start(bf16[64,1536]{1,0:T(8,128)(2,1)S(1)} %multiply_convert_fusion), channel_id=1, source_target_pairs={{0,1},{1,2},{2,3},{3,0},{4,5},{5,6},{6,7},{7,4},{8,9},{9,10},{10,1... | collective-permute-start | bytes 589832 | tf_op jit(solution)/shard_map/ppermute | solution.py:254
  88.0 13.4 %all-gather.1 = f32[4,64,8]{1,2,0:T(8,128)S(1)} all-gather(f32[1,64,8]{1,2,0:T(8,128)S(1)} %reshape.158), channel_id=1, replica_groups=mesh['seq'=8,'req'=4] {'req'}, dimensions={0}, use_global_device_ids=true | all-gather | bytes 10240 | tf_op jit(solution)/shard_map/all_gather | solution.py:259
  101.4 13.2 %all-gather = s32[4,64,8]{1,2,0:T(8,128)S(1)} all-gather(s32[1,64,8]{1,2,0:T(8,128)S(1)} %reshape.156), channel_id=1, replica_groups=mesh['seq'=8,'req'=4] {'req'}, dimensions={0}, use_global_device_ids=true | all-gather | bytes 10240 | tf_op jit(solution)/shard_map/all_gather | solution.py:258
  115.0 8.3 %collective-permute-done.1 = bf16[64,1536]{1,0:T(8,128)(2,1)S(1)} collective-permute-done((bf16[64,1536]{1,0:T(8,128)(2,1)S(1)}, bf16[64,1536]{1,0:T(8,128)(2,1)S(1)}, u32[]{:S(2)}, u32[]{:S(2)}) %collective-permute-start.1) | collective-permute-done | bytes 196640 | tf_op jit(solution)/shard_map/ppermute | solution.py:254
  123.3 7.5 %collective-permute-done.2 = bf16[64,1536]{1,0:T(8,128)(2,1)S(1)} collective-permute-done((bf16[64,1536]{1,0:T(8,128)(2,1)S(1)}, bf16[64,1536]{1,0:T(8,128)(2,1)S(1)}, u32[]{:S(2)}, u32[]{:S(2)}) %collective-permute-start.2) | collective-permute-done | bytes 196640 | tf_op jit(solution)/shard_map/ppermute | solution.py:254
  131.1 2.9 %fusion.14 = f32[256,1024]{1,0:T(8,128)S(1)} fusion(bf16[5,1536,1024]{2,1,0:T(8,128)(2,1)} %param.22, bf16[512,1536]{1,0:T(8,128)(2,1)S(1)} %constant_dynamic-update-slice_fusion, s32[]{:T(128)S(6)} %select_n.32), kind=kOutput, calls=%fused_computation.17 | convolution fusion | flops 805306368 | bytes 4980740 | tf_op jit(solution)/shard_map/dot_general | solution.py:268
  134.0 2.9 %fusion.12 = f32[256,1024]{1,0:T(8,128)S(1)} fusion(bf16[5,1536,1024]{2,1,0:T(8,128)(2,1)} %param.22, bf16[512,1536]{1,0:T(8,128)(2,1)S(1)} %constant_dynamic-update-slice_fusion, s32[]{:T(128)S(6)} %select_n.32), kind=kOutput, calls=%fused_computation.15 | convolution fusion | flops 805306368 | bytes 4980740 | tf_op jit(solution)/shard_map/dot_general | solution.py:268
  137.0 3.1 %fusion.10 = f32[256,1024]{1,0:T(8,128)S(1)} fusion(bf16[5,1536,1024]{2,1,0:T(8,128)(2,1)} %param.22, bf16[512,1536]{1,0:T(8,128)(2,1)S(1)} %constant_dynamic-update-slice_fusion, s32[]{:T(128)S(6)} %select_n.32), kind=kOutput, calls=%fused_computation.13 | convolution fusion | flops 805306368 | bytes 4980740 | tf_op jit(solution)/shard_map/dot_general | solution.py:268
  140.1 3.1 %fusion.8 = f32[256,1024]{1,0:T(8,128)S(1)} fusion(bf16[5,1536,1024]{2,1,0:T(8,128)(2,1)} %param.22, bf16[512,1536]{1,0:T(8,128)(2,1)S(1)} %constant_dynamic-update-slice_fusion, s32[]{:T(128)S(6)} %select_n.32), kind=kOutput, calls=%fused_computation.11 | convolution fusion | flops 805306368 | bytes 4980740 | tf_op jit(solution)/shard_map/dot_general | solution.py:268
  143.2 2.9 %fusion.16 = f32[256,1024]{1,0:T(8,128)S(1)} fusion(bf16[5,1536,1024]{2,1,0:T(8,128)(2,1)} %param.22, bf16[512,1536]{1,0:T(8,128)(2,1)S(1)} %constant_dynamic-update-slice_fusion, s32[]{:T(128)S(6)} %select_n.32), kind=kOutput, calls=%fused_computation.19 | convolution fusion | flops 805306368 | bytes 4980740 | tf_op jit(solution)/shard_map/dot_general | solution.py:268
  146.2 0.6 fusion.37
  146.8 0.6 fusion.35
  147.4 0.6 fusion.32
  148.0 0.6 fusion.29
  148.7 1.5 fusion.26
  150.2 3.5 %all-to-all-start.4 = ((bf16[4,64,1536]{2,1,0:T(8,128)(2,1)}), bf16[4,64,1536]{2,1,0:T(8,128)(2,1)S(1)}, u32[]{:S(2)}, u32[]{:S(2)}) async-start(bf16[4,64,1536]{2,1,0:T(8,128)(2,1)} %bitcast.41), calls=%async_computation.4 | async-start | bytes 1572864 | tf_op jit(solution)/shard_map/all_to_all | solution.py:273
  153.9 12.9 %all-to-all-done.4 = bf16[4,64,1536]{2,1,0:T(8,128)(2,1)S(1)} async-done(((bf16[4,64,1536]{2,1,0:T(8,128)(2,1)}), bf16[4,64,1536]{2,1,0:T(8,128)(2,1)S(1)}, u32[]{:S(2)}, u32[]{:S(2)}) %all-to-all-start.4) | async-done | bytes 786464 | tf_op jit(solution)/shard_map/all_to_all | solution.py:273
  166.9 0.7 add_convert_fusion
  (81 shorter events, 4.1 us)
Async XLA Ops:
  0.0 2.1 %copy-start = (bf16[2,32,1536]{2,1,0:T(8,128)(2,1)S(1)}, bf16[2,32,1536]{2,1,0:T(8,128)(2,1)}, u32[]{:S(2)}) copy-start(bf16[2,32,1536]{2,1,0:T(8,128)(2,1)} %param.17) | copy-start | bytes 589828
  0.0 1.8 %copy-start.10 = (s32[2,256]{1,0:T(2,128)S(1)}, s32[2,256]{1,0:T(2,128)}, u32[]{:S(2)}) copy-start(s32[2,256]{1,0:T(2,128)} %param.16) | copy-start | bytes 6148
  2.1 7.1 %copy-start.4 = (bf16[2,32,1536]{2,1,0:T(8,128)(2,1)S(1)}, bf16[2,32,1536]{2,1,0:T(8,128)(2,1)}, u32[]{:S(2)}) copy-start(bf16[2,32,1536]{2,1,0:T(8,128)(2,1)} %param.12) | copy-start | bytes 589828
  3.0 7.3 %copy-start.5 = (bf16[2,2,32,512]{3,2,1,0:T(8,128)(2,1)S(1)}, bf16[2,2,32,512]{3,2,1,0:T(8,128)(2,1)}, u32[]{:S(2)}) copy-start(bf16[2,2,32,512]{3,2,1,0:T(8,128)(2,1)} %param.13) | copy-start | bytes 393220
  3.0 7.6 %copy-start.3 = (bf16[2,2,256,512]{3,2,1,0:T(8,128)(2,1)S(1)}, bf16[2,2,256,512]{3,2,1,0:T(8,128)(2,1)}, u32[]{:S(2)}) copy-start(bf16[2,2,256,512]{3,2,1,0:T(8,128)(2,1)} %param.14) | copy-start | bytes 3145732
  4.1 10.2 %all-to-all-start = ((bf16[8,2,2048]{2,1,0:T(2,128)(2,1)}), bf16[8,2,2048]{2,1,0:T(2,128)(2,1)S(1)}, u32[]{:S(2)}, u32[]{:S(2)}) async-start(bf16[8,2,2048]{2,1,0:T(2,128)(2,1)} %reshape.168), calls=%async_computation | async-start | bytes 131072 | tf_op jit(solution)/shard_map/all_to_all | solution.py:210
  14.3 10.3 %all-to-all-start.2 = ((bf16[8,2,32,192]{3,2,1,0:T(8,128)(2,1)}), bf16[8,2,32,192]{3,2,1,0:T(8,128)(2,1)S(1)}, u32[]{:S(2)}, u32[]{:S(2)}) async-start(bf16[8,2,32,192]{3,2,1,0:T(8,128)(2,1)} %bitcast.115), calls=%async_computation.2 | async-start | bytes 524288 | tf_op jit(solution)/shard_map/all_to_all | solution.py:209
  19.6 8.7 %copy-start.11 = (s32[2,2]{1,0:T(2,128)S(1)}, s32[2,2]{1,0:T(2,128)}, u32[]{:S(2)}) copy-start(s32[2,2]{1,0:T(2,128)} %param.15) | copy-start | bytes 52
  24.5 20.3 %all-to-all-start.1 = ((bf16[8,2,288,128]{3,2,1,0:T(8,128)(2,1)}), bf16[8,2,288,128]{3,2,1,0:T(8,128)(2,1)S(1)}, u32[]{:S(2)}, u32[]{:S(2)}) async-start(bf16[8,2,288,128]{3,2,1,0:T(8,128)(2,1)} %copy.131), calls=%async_computation.1 | async-start | bytes 2359296 | tf_op jit(solution)/shard_map/all_to_all | solution.py:207
  50.9 0.9 copy-start.6
  50.9 1.3 copy-start.2
  59.6 8.1 %slice-start = ((bf16[2,2048,128]{1,2,0:T(8,128)(2,1)}), bf16[2,2048,64]{1,2,0:T(8,128)(2,1)S(1)}, s32[]{:S(2)}) async-start(bf16[2,2048,128]{1,2,0:T(8,128)(2,1)} %reshape.144), calls=%async_computation.5 | async-start | bytes 1048576 | tf_op jit(solution)/shard_map/slice | solution.py:225
  85.0 0.8 copy-start.7
  85.3 2.5 %copy-start.8 = (s32[2,32,8]{1,2,0:T(8,128)S(1)}, s32[2,32,8]{1,2,0:T(8,128)}, u32[]{:S(2)}) copy-start(s32[2,32,8]{1,2,0:T(8,128)} %param.20) | copy-start | bytes 6148
  85.3 2.6 %copy-start.9 = (f32[2,32,8]{1,2,0:T(8,128)S(1)}, f32[2,32,8]{1,2,0:T(8,128)}, u32[]{:S(2)}) copy-start(f32[2,32,8]{1,2,0:T(8,128)} %param.21) | copy-start | bytes 6148
  85.9 28.8 %collective-permute-start = (bf16[64,1536]{1,0:T(8,128)(2,1)S(1)}, bf16[64,1536]{1,0:T(8,128)(2,1)S(1)}, u32[]{:S(2)}, u32[]{:S(2)}) collective-permute-start(bf16[64,1536]{1,0:T(8,128)(2,1)S(1)} %multiply_convert_fusion), channel_id=1, source_target_pairs={{0,1},{1,2},{2,3},{3,0},{4,5},{5,6},{6,7},{7,4},{8,9},{9,10},{10,1... | collective-permute-start | bytes 589832 | tf_op jit(solution)/shard_map/ppermute | solution.py:254
  114.7 8.5 %collective-permute-start.1 = (bf16[64,1536]{1,0:T(8,128)(2,1)S(1)}, bf16[64,1536]{1,0:T(8,128)(2,1)S(1)}, u32[]{:S(2)}, u32[]{:S(2)}) collective-permute-start(bf16[64,1536]{1,0:T(8,128)(2,1)S(1)} %collective-permute-done), channel_id=1, source_target_pairs={{0,1},{1,2},{2,3},{3,0},{4,5},{5,6},{6,7},{7,4},{8,9},{9,10},{10,1... | collective-permute-start | bytes 589832 | tf_op jit(solution)/shard_map/ppermute | solution.py:254
  123.3 7.5 %collective-permute-start.2 = (bf16[64,1536]{1,0:T(8,128)(2,1)S(1)}, bf16[64,1536]{1,0:T(8,128)(2,1)S(1)}, u32[]{:S(2)}, u32[]{:S(2)}) collective-permute-start(bf16[64,1536]{1,0:T(8,128)(2,1)S(1)} %collective-permute-done.1), channel_id=1, source_target_pairs={{0,1},{1,2},{2,3},{3,0},{4,5},{5,6},{6,7},{7,4},{8,9},{9,10},{10,1... | collective-permute-start | bytes 589832 | tf_op jit(solution)/shard_map/ppermute | solution.py:254
  137.0 9.2 %slice-start.1 = ((s8[7864320]{0:T(1024)(128)(4,1)}), s8[4194304]{0:T(1024)(128)(4,1)S(1)}, s32[]{:S(2)}) async-start(s8[7864320]{0:T(1024)(128)(4,1)} %bitcast.131), calls=%async_computation.6 | async-start | bytes 8388608
  140.1 6.1 %slice-start.2 = ((s8[7864320]{0:T(1024)(128)(4,1)}), s8[3670016]{0:T(1024)(128)(4,1)S(1)}, s32[]{:S(2)}) async-start(s8[7864320]{0:T(1024)(128)(4,1)} %bitcast.131), calls=%async_computation.7 | async-start | bytes 7340032
  150.2 16.6 %all-to-all-start.4 = ((bf16[4,64,1536]{2,1,0:T(8,128)(2,1)}), bf16[4,64,1536]{2,1,0:T(8,128)(2,1)S(1)}, u32[]{:S(2)}, u32[]{:S(2)}) async-start(bf16[4,64,1536]{2,1,0:T(8,128)(2,1)} %bitcast.41), calls=%async_computation.4 | async-start | bytes 1572864 | tf_op jit(solution)/shard_map/all_to_all | solution.py:273
  153.7 13.9 %copy-start.1 = (bf16[2,32,1536]{2,1,0:T(8,128)(2,1)S(1)}, bf16[2,32,1536]{2,1,0:T(8,128)(2,1)}, u32[]{:S(2)}) copy-start(bf16[2,32,1536]{2,1,0:T(8,128)(2,1)} %param.17) | copy-start | bytes 589828
